TPU v7x, 32 devices: a whole 2x2x4 slice. The times are simulated.
32 devices in a mesh: ctx: 16 (over z, y, core), fs: 2 (over x).
Axes of the slice: x: 2, y: 2, z: 4, core: 2. Of those that a mesh axis runs over, the one named last changes fastest.
Arguments:
- tokens: float32 [4096, 960], P(('ctx', 'fs')), may hold values from -6 to 6
- positions: int32 [4096], P(('ctx', 'fs')), may hold values from 0 to 4095, as said below
- attn_gain: bfloat16 [960], P('fs'), may hold values from 0.099609375 to 1.8984375
- w_query: bfloat16 [960, 960], P('fs'), may hold values from -21 to 21
- w_kv: bfloat16 [960, 640], P('fs'), may hold values from -1 to 1
- w_out: bfloat16 [960, 960], P('fs'), may hold values from -3.5 to 3.5
- mlp_gain: bfloat16 [960], P('fs'), may hold values from 0.099609375 to 1.8984375
- w_gate: bfloat16 [960, 2560], P('fs'), may hold values from -0.1875 to 0.1875
- w_up: bfloat16 [960, 2560], P('fs'), may hold values from -0.1875 to 0.1875
- w_down: bfloat16 [2560, 960], P('fs'), may hold values from -0.125 to 0.125
- cotangent: float32 [4096, 960], P(('ctx', 'fs')), may hold values from -12 to 12
Outputs:
- result: float32 [4096, 960], P(('ctx', 'fs'))
- grad_tokens: float32 [4096, 960], P(('ctx', 'fs'))
- grad_attn_gain: float32 [960], P('fs')
- grad_query: float32 [960, 960], P('fs')
- grad_kv: float32 [960, 640], P('fs')
- grad_out: float32 [960, 960], P('fs')
- grad_mlp_gain: float32 [960], P('fs')
- grad_gate: float32 [960, 2560], P('fs')
- grad_up: float32 [960, 2560], P('fs')
- grad_down: float32 [2560, 960], P('fs')
Inputs may be any that keep to these rules, and one draw needn't show every extreme that they name: `positions`: a permutation of 0 to 4095 in which each aligned run of 128 entries holds consecutive rising values.
All inputs are finite; a program needn't handle non-finite values.
Results may differ from a plain program's by a relative error of at most 0.02.
Values may be sent and summed in bfloat16 or wider, within the bound.
A program may use at most 256 MiB of HBM per device.

v0:
```python
import jax
import jax.numpy as jnp
from jax import lax
from jax.sharding import PartitionSpec as P

HQ = 15
KVH = 5
HD = 64


norm_eps = 1e-05
rope_base = 10000.0
neg_large = -1e30


def rms_scale(hidden_rows):
    return lax.rsqrt(jnp.mean(hidden_rows * hidden_rows, axis=-1, keepdims=True) + norm_eps)


def rope_tables(positions):
    half_width = HD // 2
    frequency = rope_base ** (-(jnp.arange(half_width, dtype=jnp.float32) * (2.0 / HD)))
    angles = positions.astype(jnp.float32)[:, None] * frequency[None, :]
    return (jnp.cos(angles)[:, None, :], jnp.sin(angles)[:, None, :])


def rotate(values, cosine, sine_table):
    half_width = values.shape[-1] // 2
    first_half = values[..., :half_width]
    second_half = values[..., half_width:]
    return jnp.concatenate(
        [
            first_half * cosine - second_half * sine_table,
            second_half * cosine + first_half * sine_table,
        ],
        axis=-1,
    )


def norm_back(grad_gained, normed, scale_rows, gain_row):
    grad_normed = grad_gained * gain_row
    grad_gain = jnp.sum(grad_gained * normed, axis=0)
    inner_mean = jnp.mean(grad_normed * normed, axis=-1, keepdims=True)
    return (scale_rows * (grad_normed - normed * inner_mean), grad_gain)


def unchanged(carried):
    return carried


def forward_piece(carried, piece_pairs, piece_positions, query_heads, query_positions):
    length = piece_pairs.shape[0]
    width_rows = query_positions.shape[0]
    score_scale = HD ** (-0.5)
    pair_blocks = piece_pairs.reshape(length // width_rows, width_rows, piece_pairs.shape[1])
    position_blocks = piece_positions.reshape(length // width_rows, width_rows)

    def forward_visit(current_state, block_data):
        block_pairs, block_positions = block_data

        def attend(inner_state):
            row_top, row_total, accumulated = inner_state
            keys_block = block_pairs[:, : KVH * HD].reshape(width_rows, KVH, HD)
            values_block = block_pairs[:, KVH * HD :].reshape(width_rows, KVH, HD)
            scores = (
                jnp.einsum(
                    "bkgd,skd->kgbs", query_heads, keys_block, preferred_element_type=jnp.float32
                )
                * score_scale
            )
            allowed = block_positions[None, None, None, :] <= query_positions[None, None, :, None]
            masked = jnp.where(allowed, scores, neg_large)
            new_top = jnp.maximum(row_top, jnp.max(masked, axis=-1))
            soft_weights = jnp.where(allowed, jnp.exp(masked - new_top[..., None]), 0.0)
            factor = jnp.exp(row_top - new_top)
            row_total = row_total * factor + jnp.sum(soft_weights, axis=-1)
            accumulated = accumulated * factor[..., None] + jnp.einsum(
                "kgbs,skd->kgbd",
                soft_weights,
                values_block.astype(jnp.float32),
                precision=lax.Precision.HIGHEST,
            )
            return (new_top, row_total, accumulated)

        active = jnp.min(block_positions) <= jnp.max(query_positions)
        return (lax.cond(active, attend, unchanged, current_state), None)

    carried, _ = lax.scan(forward_visit, carried, (pair_blocks, position_blocks))
    return carried


def joint_grad_pass(
    all_pairs, all_positions, query_heads, dout_heads, log_heads, delta_heads, query_positions
):
    length = all_pairs.shape[0]
    width_rows = query_positions.shape[0]
    key_width = KVH * HD
    score_scale = HD ** (-0.5)
    pair_blocks = all_pairs.reshape(length // width_rows, width_rows, all_pairs.shape[1])
    position_blocks = all_positions.reshape(length // width_rows, width_rows)
    zero_block = jnp.zeros((width_rows, KVH, HD), jnp.float32)

    def joint_visit(current_state, block_data):
        block_pairs, block_positions = block_data

        def compute(inner_state):
            keys_block = block_pairs[:, :key_width].reshape(width_rows, KVH, HD)
            values_block = block_pairs[:, key_width:].reshape(width_rows, KVH, HD)
            scores = (
                jnp.einsum(
                    "bkgd,skd->kgbs", query_heads, keys_block, preferred_element_type=jnp.float32
                )
                * score_scale
            )
            allowed = block_positions[None, None, None, :] <= query_positions[None, None, :, None]
            soft_weights = jnp.where(allowed, jnp.exp(scores - log_heads[..., None]), 0.0)
            grad_soft = jnp.einsum(
                "bkgd,skd->kgbs", dout_heads, values_block, preferred_element_type=jnp.float32
            )
            grad_scores = (
                soft_weights * (grad_soft - delta_heads[..., None]) * score_scale
            ).astype(jnp.bfloat16)
            grad_query_new = inner_state + jnp.einsum(
                "kgbs,skd->kgbd", grad_scores, keys_block, preferred_element_type=jnp.float32
            )
            key_terms = jnp.einsum(
                "kgbs,bkgd->skd", grad_scores, query_heads, preferred_element_type=jnp.float32
            )
            value_terms = jnp.einsum(
                "kgbs,bkgd->skd",
                soft_weights.astype(jnp.bfloat16),
                dout_heads,
                preferred_element_type=jnp.float32,
            )
            return (grad_query_new, key_terms, value_terms)

        def skipped(inner_state):
            return (inner_state, zero_block, zero_block)

        active = jnp.min(block_positions) <= jnp.max(query_positions)
        grad_query_new, key_terms, value_terms = lax.cond(active, compute, skipped, current_state)
        terms = jnp.concatenate(
            [key_terms.reshape(width_rows, key_width), value_terms.reshape(width_rows, key_width)],
            axis=1,
        )
        return (grad_query_new, terms)

    start = jnp.zeros((KVH, HQ // KVH, query_heads.shape[0], HD), jnp.float32)
    grad_query_heads, term_blocks = lax.scan(joint_visit, start, (pair_blocks, position_blocks))
    return (grad_query_heads, term_blocks.reshape(length, 2 * key_width))


def shards(
    tokens, positions, attn_gain, w_query, w_kv, w_out, mlp_gain, w_gate, w_up, w_down, cotangent
):
    row_count = tokens.shape[0]
    groups = HQ // KVH
    query_width = HQ * HD
    key_width = KVH * HD
    gain_one, query_full, pair_full, output_full, gain_two, gate_full, upward_full, down_full = (
        lax.all_gather(attn_gain, "fs", axis=0, tiled=True),
        lax.all_gather(w_query, "fs", axis=0, tiled=True),
        lax.all_gather(w_kv, "fs", axis=0, tiled=True),
        lax.all_gather(w_out, "fs", axis=0, tiled=True),
        lax.all_gather(mlp_gain, "fs", axis=0, tiled=True),
        lax.all_gather(w_gate, "fs", axis=0, tiled=True),
        lax.all_gather(w_up, "fs", axis=0, tiled=True),
        lax.all_gather(w_down, "fs", axis=0, tiled=True),
    )
    gain_one = gain_one.astype(jnp.float32)
    gain_two = gain_two.astype(jnp.float32)
    cosine, sine_table = rope_tables(positions)
    scale_one = rms_scale(tokens)
    normed_one = tokens * scale_one
    inputs_one = (normed_one * gain_one).astype(jnp.bfloat16)
    query_linear = jnp.dot(inputs_one, query_full, preferred_element_type=jnp.float32).reshape(
        row_count, HQ, HD
    )
    queries = (
        rotate(query_linear, cosine, sine_table)
        .astype(jnp.bfloat16)
        .reshape(row_count, query_width)
    )
    pair_linear = jnp.dot(inputs_one, pair_full, preferred_element_type=jnp.float32)
    keys_rotated = rotate(
        pair_linear[:, :key_width].reshape(row_count, KVH, HD), cosine, sine_table
    ).reshape(row_count, key_width)
    key_values = jnp.concatenate([keys_rotated, pair_linear[:, key_width:]], axis=1).astype(
        jnp.bfloat16
    )
    query_heads = queries.reshape(row_count, KVH, groups, HD)
    start_state = (
        jnp.full((KVH, groups, row_count), neg_large, jnp.float32),
        jnp.zeros((KVH, groups, row_count), jnp.float32),
        jnp.zeros((KVH, groups, row_count, HD), jnp.float32),
    )
    row_top, row_total, accumulated = forward_piece(
        start_state,
        lax.all_gather(key_values, ("ctx", "fs"), axis=0, tiled=True),
        lax.all_gather(positions, ("ctx", "fs"), axis=0, tiled=True),
        query_heads,
        positions,
    )
    log_heads = row_top + jnp.log(row_total)
    head_outputs = accumulated / row_total[..., None]
    attn_rows = jnp.transpose(head_outputs, (2, 0, 1, 3)).reshape(row_count, query_width)
    attn_low = attn_rows.astype(jnp.bfloat16)
    middle = tokens + jnp.dot(attn_low, output_full, preferred_element_type=jnp.float32)
    scale_two = rms_scale(middle)
    normed_two = middle * scale_two
    inputs_two = (normed_two * gain_two).astype(jnp.bfloat16)
    gate_linear = jnp.dot(inputs_two, gate_full, preferred_element_type=jnp.float32)
    up_linear = jnp.dot(inputs_two, upward_full, preferred_element_type=jnp.float32)
    sigmoid_gate = jax.nn.sigmoid(gate_linear)
    activated = gate_linear * sigmoid_gate
    hidden = (activated * up_linear).astype(jnp.bfloat16)
    result = middle + jnp.dot(hidden, down_full, preferred_element_type=jnp.float32)
    grad_low = cotangent.astype(jnp.bfloat16)
    grad_down_w = jnp.dot(hidden.T, grad_low, preferred_element_type=jnp.float32)
    grad_hidden = jnp.dot(grad_low, down_full.T, preferred_element_type=jnp.float32)
    grad_gate_in = (
        grad_hidden * up_linear * sigmoid_gate * (1.0 + gate_linear * (1.0 - sigmoid_gate))
    ).astype(jnp.bfloat16)
    grad_up_in = (grad_hidden * activated).astype(jnp.bfloat16)
    grad_gate_w = jnp.dot(inputs_two.T, grad_gate_in, preferred_element_type=jnp.float32)
    grad_upward_w = jnp.dot(inputs_two.T, grad_up_in, preferred_element_type=jnp.float32)
    grad_inputs_two = jnp.dot(
        grad_gate_in, gate_full.T, preferred_element_type=jnp.float32
    ) + jnp.dot(grad_up_in, upward_full.T, preferred_element_type=jnp.float32)
    grad_norm_two, grad_mlp_gain = norm_back(grad_inputs_two, normed_two, scale_two, gain_two)
    grad_middle = cotangent + grad_norm_two
    grad_middle_low = grad_middle.astype(jnp.bfloat16)
    grad_output_w = jnp.dot(attn_low.T, grad_middle_low, preferred_element_type=jnp.float32)
    grad_attn = jnp.dot(grad_middle_low, output_full.T, preferred_element_type=jnp.float32).astype(
        jnp.bfloat16
    )
    delta_rows = jnp.sum(
        grad_attn.astype(jnp.float32).reshape(row_count, HQ, HD)
        * attn_rows.reshape(row_count, HQ, HD),
        axis=-1,
    )
    delta_heads = jnp.transpose(delta_rows.reshape(row_count, KVH, groups), (1, 2, 0))
    dout_heads = grad_attn.reshape(row_count, KVH, groups, HD)
    all_pairs, all_positions = (
        lax.all_gather(key_values, ("ctx", "fs"), axis=0, tiled=True),
        lax.all_gather(positions, ("ctx", "fs"), axis=0, tiled=True),
    )
    grad_query_heads, term_rows = joint_grad_pass(
        all_pairs, all_positions, query_heads, dout_heads, log_heads, delta_heads, positions
    )
    summed = lax.psum_scatter(term_rows, ("ctx", "fs"), scatter_dimension=0, tiled=True)
    grad_keys = summed[:, :key_width].reshape(row_count, KVH, HD)
    grad_values = summed[:, key_width:].reshape(row_count, KVH, HD)
    grad_query_rows = jnp.transpose(grad_query_heads, (2, 0, 1, 3)).reshape(row_count, HQ, HD)
    query_back = (
        rotate(grad_query_rows, cosine, -sine_table)
        .astype(jnp.bfloat16)
        .reshape(row_count, query_width)
    )
    key_back = rotate(grad_keys, cosine, -sine_table).reshape(row_count, key_width)
    pair_back = jnp.concatenate(
        [key_back, grad_values.reshape(row_count, key_width)], axis=1
    ).astype(jnp.bfloat16)
    grad_query_w = jnp.dot(inputs_one.T, query_back, preferred_element_type=jnp.float32)
    grad_pair_w = jnp.dot(inputs_one.T, pair_back, preferred_element_type=jnp.float32)
    grad_inputs_one = jnp.dot(
        query_back, query_full.T, preferred_element_type=jnp.float32
    ) + jnp.dot(pair_back, pair_full.T, preferred_element_type=jnp.float32)
    grad_norm_one, grad_attn_gain = norm_back(grad_inputs_one, normed_one, scale_one, gain_one)
    grad_tokens = grad_middle + grad_norm_one
    halves = (
        lax.psum_scatter(
            grad_attn_gain.astype(jnp.bfloat16), "fs", scatter_dimension=0, tiled=True
        ).astype(jnp.float32),
        lax.psum_scatter(
            grad_query_w.astype(jnp.bfloat16), "fs", scatter_dimension=0, tiled=True
        ).astype(jnp.float32),
        lax.psum_scatter(
            grad_pair_w.astype(jnp.bfloat16), "fs", scatter_dimension=0, tiled=True
        ).astype(jnp.float32),
        lax.psum_scatter(
            grad_output_w.astype(jnp.bfloat16), "fs", scatter_dimension=0, tiled=True
        ).astype(jnp.float32),
        lax.psum_scatter(
            grad_mlp_gain.astype(jnp.bfloat16), "fs", scatter_dimension=0, tiled=True
        ).astype(jnp.float32),
        lax.psum_scatter(
            grad_gate_w.astype(jnp.bfloat16), "fs", scatter_dimension=0, tiled=True
        ).astype(jnp.float32),
        lax.psum_scatter(
            grad_upward_w.astype(jnp.bfloat16), "fs", scatter_dimension=0, tiled=True
        ).astype(jnp.float32),
        lax.psum_scatter(
            grad_down_w.astype(jnp.bfloat16), "fs", scatter_dimension=0, tiled=True
        ).astype(jnp.float32),
    )
    slices = (
        lax.psum_scatter(halves[1], "ctx", scatter_dimension=1, tiled=True),
        lax.psum_scatter(halves[2], "ctx", scatter_dimension=1, tiled=True),
        lax.psum_scatter(halves[3], "ctx", scatter_dimension=1, tiled=True),
        lax.psum_scatter(halves[5], "ctx", scatter_dimension=1, tiled=True),
        lax.psum_scatter(halves[6], "ctx", scatter_dimension=1, tiled=True),
        lax.psum_scatter(halves[7], "ctx", scatter_dimension=1, tiled=True),
    )
    spread = (
        lax.all_gather(slices[0].astype(jnp.bfloat16), "ctx", axis=1, tiled=True).astype(
            jnp.float32
        ),
        lax.all_gather(slices[1].astype(jnp.bfloat16), "ctx", axis=1, tiled=True).astype(
            jnp.float32
        ),
        lax.all_gather(slices[2].astype(jnp.bfloat16), "ctx", axis=1, tiled=True).astype(
            jnp.float32
        ),
        lax.all_gather(slices[3].astype(jnp.bfloat16), "ctx", axis=1, tiled=True).astype(
            jnp.float32
        ),
        lax.all_gather(slices[4].astype(jnp.bfloat16), "ctx", axis=1, tiled=True).astype(
            jnp.float32
        ),
        lax.all_gather(slices[5].astype(jnp.bfloat16), "ctx", axis=1, tiled=True).astype(
            jnp.float32
        ),
    )
    gain_grads = lax.psum((halves[0], halves[4]), "ctx")
    return (
        result,
        grad_tokens,
        gain_grads[0],
        spread[0],
        spread[1],
        spread[2],
        gain_grads[1],
        spread[3],
        spread[4],
        spread[5],
    )


def solution(mesh):
    in_specs = (
        P(("ctx", "fs"), None),
        P(("ctx", "fs")),
        P("fs"),
        P("fs", None),
        P("fs", None),
        P("fs", None),
        P("fs"),
        P("fs", None),
        P("fs", None),
        P("fs", None),
        P(("ctx", "fs"), None),
    )
    out_specs = (
        P(("ctx", "fs"), None),
        P(("ctx", "fs"), None),
        P("fs"),
        P("fs", None),
        P("fs", None),
        P("fs", None),
        P("fs"),
        P("fs", None),
        P("fs", None),
        P("fs", None),
    )
    return jax.shard_map(shards, mesh=mesh, in_specs=in_specs, out_specs=out_specs, check_vma=False)
```

profile of v0, /device:TPU:0, one launch (start us, length us, event | category | flops | bytes accessed | tf_op | source)
XLA Modules:
  0.0 1518.4 jit_solution(13740855633039782844)
XLA Ops:
  12.5 5.8 all-reduce.11
  21.3 14.3 all-gather.15.cloned.1.call-done
  41.1 69.6 %all-gather = s32[32,1,128]{2,1,0:T(1,128)} all-gather(s32[1,1,128]{2,1,0:T(1,128)} %bitcast.28), channel_id=1, replica_groups=mesh['ctx'=16,'fs'=2] {'ctx','fs'}, dimensions={0}, use_global_device_ids=true | all-gather | bytes 16896 | tf_op jit(solution)/shard_map/all_gather | solution.py:200
  113.3 24.5 %all-gather.17.cloned.1.call-done = bf16[4096,640]{1,0:T(8,128)(2,1)} async-done(((bf16[128,640]{1,0:T(8,128)(2,1)}), bf16[4096,640]{1,0:T(8,128)(2,1)}) %all-gather.17.cloned.1.call-update) | async-done | bytes 5242896 | tf_op jit(solution)/shard_map/all_gather | solution.py:199
  137.8 7.9 copy.72
  145.7 91.4 %while.31 = (s32[]{:T(128)}, f32[5,3,128]{2,1,0:T(4,128)S(1)}, f32[5,3,128]{2,1,0:T(4,128)S(1)}, f32[5,3,128,64]{2,3,1,0:T(8,128)S(1)}, s32[32,128]{1,0:T(8,128)...) while((s32[]{:T(128)}, f32[5,3,128]{2,1,0:T(4,128)S(1)}, ...), condition=%wide.region_8.9_spmd, body=%wide.region_2.8_spmd.sunk | while | flops 222433152 | bytes 5187839 | solution.py:88
  245.3 56.6 %all-gather.25.cloned.1.call-done = bf16[960,2560]{1,0:T(8,128)(2,1)} async-done(((bf16[480,2560]{1,0:T(8,128)(2,1)}), bf16[960,2560]{1,0:T(8,128)(2,1)}) %all-gather.25.cloned.1.call-update) | async-done | bytes 4915216 | tf_op jit(solution)/shard_map/all_gather | solution.py:167
  306.2 62.1 %all-gather.27.cloned.1.call-done = bf16[2560,960]{0,1:T(8,128)(2,1)} async-done(((bf16[1280,960]{0,1:T(8,128)(2,1)}), bf16[2560,960]{0,1:T(8,128)(2,1)}) %all-gather.27.cloned.1.call-update) | async-done | bytes 4915216 | tf_op jit(solution)/shard_map/all_gather | solution.py:168
  392.2 123.3 %while.32 = (s32[]{:T(128)}, f32[5,3,128,64]{2,3,1,0:T(8,128)S(1)}, f32[32,128,640]{2,1,0:T(8,128)}, s32[32,128]{1,0:T(8,128)}, s32[]{:T(128)}, /*index=5*/s32[1...) while((s32[]{:T(128)}, f32[5,3,128,64]{2,3,1,0:T(8,128)S(1)}, ...), condition=%wide.region_16.17_spmd, body=%wide.region_12.0_spmd.sunk | while | flops 159473792 | bytes 9635575 | solution.py:149
  534.1 112.2 %reduce-scatter.23.cloned.1.call-done = bf16[480,960]{1,0:T(8,128)(2,1)} async-done(((bf16[960,960]{1,0:T(8,128)(2,1)}), bf16[480,960]{1,0:T(8,128)(2,1)}) %reduce-scatter.23.cloned.1.call-update) | async-done | bytes 921616 | tf_op jit(solution)/shard_map/reduce_scatter | solution.py:275
  646.3 33.3 %reduce-scatter.27.cloned.1.call-done = bf16[480,960]{1,0:T(8,128)(2,1)} async-done(((bf16[960,960]{1,0:T(8,128)(2,1)}), bf16[480,960]{1,0:T(8,128)(2,1)}) %reduce-scatter.27.cloned.1.call-update) | async-done | bytes 921616 | tf_op jit(solution)/shard_map/reduce_scatter | solution.py:281
  679.7 64.9 %reduce-scatter.33.cloned.1.call-done = bf16[1280,960]{0,1:T(8,128)(2,1)} async-done(((bf16[2560,960]{0,1:T(8,128)(2,1)}), bf16[1280,960]{0,1:T(8,128)(2,1)}) %reduce-scatter.33.cloned.1.call-update) | async-done | bytes 2457616 | tf_op jit(solution)/shard_map/reduce_scatter | solution.py:293
  748.9 224.7 %reduce-scatter.21.cloned.1.call-done = f32[128,640]{1,0:T(8,128)} async-done(((f32[4096,640]{1,0:T(8,128)}), f32[128,640]{1,0:T(8,128)}) %reduce-scatter.21.cloned.1.call-update) | async-done | bytes 327696 | tf_op jit(solution)/shard_map/reduce_scatter | solution.py:251
  977.5 81.4 %fusion = f32[1280,64]{0,1:T(8,128)} fusion(f32[1280,960]{0,1:T(8,128)} %convert_element_type.189), kind=kCustom, calls=%all-reduce-scatter | all-reduce-scatter fusion | flops 1310721 | bytes 5243392
  1068.4 10.3 reduce-scatter.37.cloned.1.call-done
  1080.5 79.6 %reduce-scatter.39.cloned.1.call-done = f32[160,480]{1,0:T(8,128)} async-done(((f32[2560,480]{1,0:T(8,128)}), f32[160,480]{1,0:T(8,128)}) %reduce-scatter.39.cloned.1.call-update) | async-done | bytes 307216
  1170.3 89.8 %all-reduce.14.cloned.1.call-done = (bf16[480,960]{1,0:T(8,128)(2,1)}, bf16[480,960]{1,0:T(8,128)(2,1)}) async-done(((bf16[480,960]{1,0:T(8,128)(2,1)}, bf16[480,960]{1,0:T(8,128)(2,1)}), (bf16[480,960]{1,0:T(8,128)(2,1)}, bf16[480,960]{1,0:T(8,128)(2,1)})) %all-reduce.14.cloned.1.call-update) | async-done | bytes 1843216
  1261.3 22.8 %reduce-scatter.25.cloned.1.call-done = bf16[480,640]{1,0:T(8,128)(2,1)} async-done(((bf16[960,640]{1,0:T(8,128)(2,1)}), bf16[480,640]{1,0:T(8,128)(2,1)}) %reduce-scatter.25.cloned.1.call-update) | async-done | bytes 614416 | tf_op jit(solution)/shard_map/reduce_scatter | solution.py:278
  1286.6 28.1 %all-gather.1 = bf16[16,60,480]{2,1,0:T(8,128)(2,1)} all-gather(bf16[1,60,480]{2,1,0:T(8,128)(2,1)S(1)} %copy.77), channel_id=1, replica_groups=mesh['ctx'=16,'fs'=2] {'ctx'}, dimensions={0}, use_global_device_ids=true | all-gather | bytes 979200 | tf_op jit(solution)/shard_map/all_gather | solution.py:306
  1319.2 23.8 %all-gather.2 = bf16[16,60,480]{2,1,0:T(8,128)(2,1)} all-gather(bf16[1,60,480]{2,1,0:T(8,128)(2,1)S(1)} %copy.79), channel_id=1, replica_groups=mesh['ctx'=16,'fs'=2] {'ctx'}, dimensions={0}, use_global_device_ids=true | all-gather | bytes 979200 | tf_op jit(solution)/shard_map/all_gather | solution.py:312
  1356.8 32.5 %all-reduce.8 = (f32[480]{0:T(512)}, f32[480]{0:T(512)}) all-reduce(f32[480]{0:T(512)S(1)} %dynamic-slice_convert_fusion.4, f32[480]{0:T(512)S(1)} %dynamic-slice_convert_fusion.3), channel_id=1, replica_groups=mesh['ctx'=16,'fs'=2] {'ctx'}, use_global_device_ids=true, to_apply=%region_21.22 | all-reduce | flops 960 | bytes 7680 | tf_op jit(solution)/shard_map/psum | solution.py:325
  1395.2 31.9 %all-gather.31.cloned.1.call-done = bf16[480,2560]{0,1:T(8,128)(2,1)} async-done(((bf16[480,160]{0,1:T(8,128)(2,1)}), bf16[480,2560]{0,1:T(8,128)(2,1)}) %all-gather.31.cloned.1.call-update) | async-done | bytes 2457616 | tf_op jit(solution)/shard_map/all_gather | solution.py:318
  1431.9 56.3 %reduce-scatter.35.cloned.1.call-done = f32[40,480]{1,0:T(8,128)} async-done(((f32[640,480]{1,0:T(8,128)}), f32[40,480]{1,0:T(8,128)}) %reduce-scatter.35.cloned.1.call-update) | async-done | bytes 76816
  1489.1 21.2 %all_gather.61 = bf16[480,640]{0,1:T(8,128)(2,1)S(1)} all-gather(bf16[480,40]{0,1:T(8,128)(2,1)S(1)} %bitcast_convert_fusion.3), channel_id=1, replica_groups=mesh['ctx'=16,'fs'=2] {'ctx'}, dimensions={1}, use_global_device_ids=true | all-gather | bytes 652800 | tf_op jit(solution)/shard_map/all_gather | solution.py:309
  (501 shorter events, 276.2 us)
Async XLA Ops:
  7.2 28.4 %all-gather.15.cloned.1.call-start = ((), (), s32[]{:S(2)}) async-start(), calls=%async_computation.10 | async-start | bytes 1843200 | tf_op jit(solution)/shard_map/all_gather | solution.py:163
  7.9 102.8 %all-gather.19.cloned.1.call-start = ((), (), s32[]{:S(2)}) async-start(), calls=%async_computation.12 | async-start | bytes 2949120 | tf_op jit(solution)/shard_map/all_gather | solution.py:162
  8.7 129.1 %all-gather.17.cloned.1.call-start = ((), (), s32[]{:S(2)}) async-start(), calls=%async_computation.11 | async-start | bytes 5406720 | tf_op jit(solution)/shard_map/all_gather | solution.py:199
  38.5 199.5 %all-gather.21.cloned.1.call-start = ((), (), s32[]{:S(2)}) async-start(), calls=%async_computation.13 | async-start | bytes 2949120 | tf_op jit(solution)/shard_map/all_gather | solution.py:164
  39.1 201.6 %all-gather.23.cloned.1.call-start = ((), (), s32[]{:S(2)}) async-start(), calls=%async_computation.14 | async-start | bytes 7372800 | tf_op jit(solution)/shard_map/all_gather | solution.py:166
  39.7 262.2 %all-gather.25.cloned.1.call-start = ((), (), s32[]{:S(2)}) async-start(), calls=%async_computation.15 | async-start | bytes 7372800 | tf_op jit(solution)/shard_map/all_gather | solution.py:167
  40.3 328.0 %all-gather.27.cloned.1.call-start = ((), (), s32[]{:S(2)}) async-start(), calls=%async_computation.16 | async-start | bytes 7372800 | tf_op jit(solution)/shard_map/all_gather | solution.py:168
  41.0 483.2 %reduce-scatter.29.cloned.1.call-start = ((), (), s32[]{:S(2)}) async-start(), calls=%async_computation.21 | async-start | bytes 7372800 | tf_op jit(solution)/shard_map/reduce_scatter | solution.py:287
  245.2 123.0 %copy-start.4 = (f32[128,960]{0,1:T(8,128)S(1)}, f32[128,960]{0,1:T(8,128)}, u32[]{:S(2)}) copy-start(f32[128,960]{0,1:T(8,128)} %param.29) | copy-start | bytes 1474564
  377.6 151.6 %reduce-scatter.31.cloned.1.call-start = ((), (), s32[]{:S(2)}) async-start(), calls=%async_computation.23 | async-start | bytes 7372800 | tf_op jit(solution)/shard_map/reduce_scatter | solution.py:290
  392.1 254.2 %reduce-scatter.23.cloned.1.call-start = ((), (), s32[]{:S(2)}) async-start(), calls=%async_computation.18 | async-start | bytes 2949120 | tf_op jit(solution)/shard_map/reduce_scatter | solution.py:275
  517.6 162.0 %reduce-scatter.27.cloned.1.call-start = ((), (), s32[]{:S(2)}) async-start(), calls=%async_computation.20 | async-start | bytes 2949120 | tf_op jit(solution)/shard_map/reduce_scatter | solution.py:281
  519.6 225.0 %reduce-scatter.33.cloned.1.call-start = ((), (), s32[]{:S(2)}) async-start(), calls=%async_computation.25 | async-start | bytes 7372800 | tf_op jit(solution)/shard_map/reduce_scatter | solution.py:293
  523.4 450.2 %reduce-scatter.21.cloned.1.call-start = ((), (), s32[]{:S(2)}) async-start(), calls=%async_computation.17 | async-start | bytes 10813440 | tf_op jit(solution)/shard_map/reduce_scatter | solution.py:251
  524.1 554.6 %reduce-scatter.37.cloned.1.call-start = ((), (), s32[]{:S(2)}) async-start(), calls=%async_computation.28 | async-start | bytes 5570560
  529.1 630.9 %reduce-scatter.39.cloned.1.call-start = ((), (), s32[]{:S(2)}) async-start(), calls=%async_computation.29 | async-start | bytes 5570560
  534.0 726.1 %all-reduce.14.cloned.1.call-start = ((), (), s32[]{:S(2)}) async-start(), calls=%async_computation.30 | async-start | bytes 3932160
  679.7 604.5 %reduce-scatter.25.cloned.1.call-start = ((), (), s32[]{:S(2)}) async-start(), calls=%async_computation.19 | async-start | bytes 1843200 | tf_op jit(solution)/shard_map/reduce_scatter | solution.py:278
  977.4 368.9 %all-gather.33.cloned.1.call-start = ((), (), s32[]{:S(2)}) async-start(), calls=%async_computation.26 | async-start | bytes 2785280 | tf_op jit(solution)/shard_map/all_gather | solution.py:321
  1058.9 104.3 %copy-start.1 = (bf16[960,960]{1,0:T(8,128)(2,1)S(1)}, bf16[960,960]{1,0:T(8,128)(2,1)}, u32[]{:S(2)}) copy-start(bf16[960,960]{1,0:T(8,128)(2,1)} %all-gather.19.cloned.1.call-done) | copy-start | bytes 5529604
  1060.7 2.6 collective-permute-start
  1068.3 322.0 %all-gather.29.cloned.1.call-start = ((), (), s32[]{:S(2)}) async-start(), calls=%async_computation.22 | async-start | bytes 2785280 | tf_op jit(solution)/shard_map/all_gather | solution.py:315
  1080.4 346.7 %all-gather.31.cloned.1.call-start = ((), (), s32[]{:S(2)}) async-start(), calls=%async_computation.24 | async-start | bytes 2785280 | tf_op jit(solution)/shard_map/all_gather | solution.py:318
  1161.7 326.5 %reduce-scatter.35.cloned.1.call-start = ((), (), s32[]{:S(2)}) async-start(), calls=%async_computation.27 | async-start | bytes 1392640
  (20 other events, 102.4 us)
Sparse Core Ops, SparseCore 0:
  9.5 26.0 all-gather.14
  37.1 31.7 all-gather.18
  72.3 65.3 all-gather.16
  139.2 30.1 all-gather.20
  170.7 64.8 all-gather.22
  237.0 64.8 all-gather.24
  303.4 64.8 all-gather.26
  377.7 62.1 reduce-scatter.28
  442.8 62.1 reduce-scatter.30
  517.7 128.5 reduce-scatter.22
  649.1 30.4 reduce-scatter.26
  682.4 62.1 reduce-scatter.32
  746.9 226.6 reduce-scatter.20
  977.3 101.3 reduce-scatter.36
  1082.4 77.5 reduce-scatter.38
  1163.5 96.6 all-reduce.13
  1262.8 21.2 reduce-scatter.24
  1286.9 50.9 all-gather.32
  1340.7 42.1 all-gather.28
  1385.1 41.9 all-gather.30
  1430.7 57.4 reduce-scatter.34
where the time goes:
time: 1530 us; the launch traced here: 1520 us
  waiting for transfers between devices  888 us (58%)
  blocking collectives  267 us (17%)
  other arithmetic  104 us (7%)
  local copies, waits for them, and re-layouts  91.7 us (6%)
  loops' own time  86.4 us (6%)
  matrix products  60.7 us (4%)
  between operations  17.3 us (1%)
    unnamed x26, waiting for transfers between devices  241 us
    reduce_scatter x1, waiting for transfers between devices, shards(): lax.psum_scatter(term_rows, ('ctx', 'fs'), scatter_dimension=0, tiled=True)  225 us
    reduce_scatter x1, waiting for transfers between devices, shards(): lax.psum_scatter(grad_query_w.astype(jnp.bfloat16), 'fs', scatter_dimensi...  112 us
    unnamed x3, blocking collectives  92.2 us
    all_gather x1, blocking collectives, shards(): lax.all_gather(positions, ('ctx', 'fs'), axis=0, tiled=True)  69.6 us
    reduce_scatter x1, waiting for transfers between devices, shards(): lax.psum_scatter(grad_down_w.astype(jnp.bfloat16), 'fs', scatter_dimensio...  64.9 us
    all_gather x1, waiting for transfers between devices, shards(): lax.all_gather(w_down, 'fs', axis=0, tiled=True)  62.1 us
    all_gather x1, waiting for transfers between devices, shards(): lax.all_gather(w_up, 'fs', axis=0, tiled=True)  56.6 us
  transfers between devices with their start and end apart: 22, of which 15 were waited for; matrix products, arithmetic and copies ran while one was open for 21% of the time, Pallas kernels for 0%

commit v1 on v0

v1 whole, which is shorter than its diff:
```python
import functools

import jax
import jax.numpy as jnp
from jax import lax
from jax.experimental import pallas as pl
from jax.experimental.pallas import tpu as pltpu
from jax.sharding import PartitionSpec as P

HQ = 15
KVH = 5
HD = 64


norm_eps = 1e-05
rope_base = 10000.0
neg_large = -1e30
AXES = ("chip", "core", "fs")
CTX = ("chip", "core")
SWAP = [(0, 1), (1, 0)]


def rms_scale(hidden_rows):
    return lax.rsqrt(jnp.mean(hidden_rows * hidden_rows, axis=-1, keepdims=True) + norm_eps)


def rope_tables(positions):
    half_width = HD // 2
    frequency = rope_base ** (-(jnp.arange(half_width, dtype=jnp.float32) * (2.0 / HD)))
    angles = positions.astype(jnp.float32)[:, None] * frequency[None, :]
    return (jnp.cos(angles)[:, None, :], jnp.sin(angles)[:, None, :])


def rotate(values, cosine, sine_table):
    half_width = values.shape[-1] // 2
    first_half = values[..., :half_width]
    second_half = values[..., half_width:]
    return jnp.concatenate(
        [
            first_half * cosine - second_half * sine_table,
            second_half * cosine + first_half * sine_table,
        ],
        axis=-1,
    )


def norm_back(grad_gained, normed, scale_rows, gain_row):
    grad_normed = grad_gained * gain_row
    grad_gain = jnp.sum(grad_gained * normed, axis=0)
    inner_mean = jnp.mean(grad_normed * normed, axis=-1, keepdims=True)
    return (scale_rows * (grad_normed - normed * inner_mean), grad_gain)


TILE = 128


def chunk_of(blocks):
    for size in (4, 2):
        if blocks % size == 0:
            return size
    return 1


def load_chunk(pairs_ref, slots_ref, first, chunk, lane):
    parts = []
    for step in range(chunk):
        row = pl.multiple_of(slots_ref[first + step] * TILE, TILE)
        parts.append(pairs_ref[pl.ds(row, TILE), lane * 128 : (lane + 1) * 128])
    return parts[0] if chunk == 1 else jnp.concatenate(parts, axis=0)


def allowed_mask(first, chunk, block, width):
    rows = lax.broadcasted_iota(jnp.int32, (chunk * TILE, width), 0) + first * TILE
    columns = lax.broadcasted_iota(jnp.int32, (chunk * TILE, width), 1) % TILE + block * TILE
    return rows <= columns


NT = (((1,), (1,)), ((), ()))


def forward_kernel(chunk, slots_ref, own_ref, query_ref, pairs_ref, out_ref, log_ref, top_ref, total_ref):
    block = own_ref[0]
    width = query_ref.shape[1]
    out_ref[...] = jnp.zeros_like(out_ref)
    top_ref[...] = jnp.full_like(top_ref, neg_large)
    total_ref[...] = jnp.zeros_like(total_ref)
    score_scale = HD ** (-0.5)

    def visit(index, masked):
        first = index * chunk
        loaded = [load_chunk(pairs_ref, slots_ref, first, chunk, lane) for lane in range(KVH)]
        flipped = {lane: loaded[lane].T for lane in range(KVH // 2, KVH)}
        if masked:
            allowed = allowed_mask(first, chunk, block, width)
        for head in range(KVH):
            scores = score_scale * lax.dot_general(
                loaded[head // 2], query_ref[head], NT, preferred_element_type=jnp.float32
            )
            if masked:
                scores = jnp.where(allowed, scores, neg_large)
            top = top_ref[head]
            new_top = jnp.maximum(top, jnp.max(scores, axis=0, keepdims=True))
            weights = jnp.exp(scores - new_top)
            factor = jnp.exp(top - new_top)
            top_ref[head] = new_top
            total_ref[head] = total_ref[head] * factor + jnp.sum(weights, axis=0, keepdims=True)
            high = weights.astype(jnp.bfloat16)
            low = (weights - high.astype(jnp.float32)).astype(jnp.bfloat16)
            values = flipped[(KVH + head) // 2]
            out_ref[head] = (
                out_ref[head] * factor
                + jnp.dot(values, high, preferred_element_type=jnp.float32)
                + jnp.dot(values, low, preferred_element_type=jnp.float32)
            )

    whole = block // chunk
    lax.fori_loop(0, whole, lambda i, c: (visit(i, False), c)[1], 0)
    visit(whole, True)
    for head in range(KVH):
        total = total_ref[head]
        out_ref[head] = out_ref[head] / total
        log_ref[head] = top_ref[head] + jnp.log(total)


def backward_kernel(
    chunk, slots_ref, own_ref, query_ref, dout_ref, log_ref, delta_ref, pairs_ref, grad_ref, terms_ref
):
    block = own_ref[0]
    width = query_ref.shape[1]
    grad_ref[...] = jnp.zeros_like(grad_ref)
    score_scale = HD ** (-0.5)
    rows = chunk * TILE

    def visit(index, masked):
        first = index * chunk
        loaded = [load_chunk(pairs_ref, slots_ref, first, chunk, lane) for lane in range(KVH)]
        flipped = {lane: loaded[lane].T for lane in range((KVH + 1) // 2)}
        if masked:
            allowed = allowed_mask(first, chunk, block, width)
        sums = [None] * KVH

        def add(lane, term):
            sums[lane] = term if sums[lane] is None else sums[lane] + term

        for head in range(KVH):
            key_lane, value_lane = head // 2, (KVH + head) // 2
            scores = score_scale * lax.dot_general(
                loaded[key_lane], query_ref[head], NT, preferred_element_type=jnp.float32
            )
            if masked:
                scores = jnp.where(allowed, scores, neg_large)
            weights = jnp.exp(scores - log_ref[head])
            grad_soft = lax.dot_general(
                loaded[value_lane], dout_ref[head], NT, preferred_element_type=jnp.float32
            )
            grad_scores = (weights * (grad_soft - delta_ref[head]) * score_scale).astype(
                jnp.bfloat16
            )
            grad_ref[head] += jnp.dot(
                flipped[key_lane], grad_scores, preferred_element_type=jnp.float32
            )
            add(
                key_lane,
                jnp.dot(grad_scores, query_ref[head], preferred_element_type=jnp.float32),
            )
            add(
                value_lane,
                jnp.dot(
                    weights.astype(jnp.bfloat16),
                    dout_ref[head],
                    preferred_element_type=jnp.float32,
                ),
            )
        for lane in range(KVH):
            for step in range(chunk):
                row = pl.multiple_of(slots_ref[first + step] * TILE, TILE)
                terms_ref[pl.ds(row, TILE), lane * 128 : (lane + 1) * 128] = sums[lane][
                    step * TILE : (step + 1) * TILE
                ].astype(terms_ref.dtype)

    whole = block // chunk
    lax.fori_loop(0, whole, lambda i, c: (visit(i, False), c)[1], 0)
    visit(whole, True)

    def clear(index, carry):
        row = pl.multiple_of(slots_ref[index] * TILE, TILE)
        terms_ref[pl.ds(row, TILE), :] = jnp.zeros((TILE, terms_ref.shape[1]), terms_ref.dtype)
        return carry

    lax.fori_loop((whole + 1) * chunk, slots_ref.shape[0], clear, 0)


def attend(query_pad, pairs, slots, own):
    heads, width, lanes = query_pad.shape
    length = pairs.shape[0]
    smem = pl.BlockSpec(memory_space=pltpu.SMEM)
    vmem = pl.BlockSpec(memory_space=pltpu.VMEM)
    return pl.pallas_call(
        functools.partial(forward_kernel, chunk_of(length // TILE)),
        out_shape=(
            jax.ShapeDtypeStruct((heads, lanes, width), jnp.float32),
            jax.ShapeDtypeStruct((heads, 1, width), jnp.float32),
        ),
        in_specs=[smem, smem, vmem, vmem],
        out_specs=(vmem, vmem),
        scratch_shapes=[
            pltpu.VMEM((heads, 1, width), jnp.float32),
            pltpu.VMEM((heads, 1, width), jnp.float32),
        ],
        compiler_params=pltpu.CompilerParams(vmem_limit_bytes=56 * 2**20),
        cost_estimate=pl.CostEstimate(
            flops=6 * heads * width * length * lanes,
            bytes_accessed=2 * pairs.size,
            transcendentals=heads * width * length,
        ),
        name="attend",
    )(slots, own, query_pad, pairs)


def attend_back(query_pad, dout_pad, logs, deltas, pairs, slots, own):
    heads, width, lanes = query_pad.shape
    length = pairs.shape[0]
    smem = pl.BlockSpec(memory_space=pltpu.SMEM)
    vmem = pl.BlockSpec(memory_space=pltpu.VMEM)
    return pl.pallas_call(
        functools.partial(backward_kernel, chunk_of(length // TILE)),
        out_shape=(
            jax.ShapeDtypeStruct((heads, lanes, width), jnp.float32),
            jax.ShapeDtypeStruct(pairs.shape, jnp.bfloat16),
        ),
        in_specs=[smem, smem, vmem, vmem, vmem, vmem, vmem],
        out_specs=(vmem, vmem),
        compiler_params=pltpu.CompilerParams(vmem_limit_bytes=56 * 2**20),
        cost_estimate=pl.CostEstimate(
            flops=10 * heads * width * length * lanes,
            bytes_accessed=4 * pairs.size,
            transcendentals=heads * width * length,
        ),
        name="attend_back",
    )(slots, own, query_pad, dout_pad, logs, deltas, pairs)


def pad_heads(rows, first_half):
    count = rows.shape[0]
    groups = HQ // KVH
    heads = jnp.transpose(rows.reshape(count, KVH, groups, HD), (1, 2, 0, 3)).reshape(
        KVH, groups * count, HD
    )
    empty = jnp.zeros_like(heads)
    odd = ((jnp.arange(KVH) + first_half) % 2 == 1)[:, None, None]
    return jnp.concatenate([jnp.where(odd, empty, heads), jnp.where(odd, heads, empty)], axis=2)


def unpad_heads(padded, first_half):
    groups = HQ // KVH
    count = padded.shape[2] // groups
    odd = ((jnp.arange(KVH) + first_half) % 2 == 1)[:, None, None]
    heads = jnp.where(odd, padded[:, HD:], padded[:, :HD])
    return jnp.transpose(heads.reshape(KVH, HD, groups, count), (3, 0, 2, 1)).reshape(
        count, HQ * HD
    )


def spread_weight(part):
    cores = lax.axis_size("core")
    rows = part.shape[0] // cores
    own = lax.dynamic_slice_in_dim(part, lax.axis_index("core") * rows, rows, axis=0)
    return lax.all_gather(own, ("fs", "core"), axis=0, tiled=True)


def swap_whole(rows):
    return jnp.concatenate([rows, lax.ppermute(rows, "fs", SWAP)], axis=0)


def swap_tokens(rows, unit):
    half = rows.shape[1] // 2
    unit = unit * lax.axis_size(CTX)
    extra = -half % unit
    first, second = (
        jnp.pad(piece, ((0, 0), (0, extra))) for piece in (rows[:, :half], rows[:, half:])
    )
    lower = lax.axis_index("fs") == 0
    mine, theirs = jnp.where(lower, first, second), jnp.where(lower, second, first)
    return jnp.concatenate([mine, lax.ppermute(theirs, "fs", SWAP)], axis=0)


def ctx_scatter(left, right):
    partial = jnp.dot(left.T, right, preferred_element_type=jnp.float32).astype(jnp.bfloat16)
    return lax.psum_scatter(partial, CTX, scatter_dimension=0, tiled=True)


def ctx_gather(piece, rows):
    return lax.all_gather(piece, CTX, axis=0, tiled=True)[:rows].astype(jnp.float32)


def shards(
    tokens, positions, attn_gain, w_query, w_kv, w_out, mlp_gain, w_gate, w_up, w_down, cotangent
):
    row_count = tokens.shape[0]
    groups = HQ // KVH
    query_width = HQ * HD
    key_width = KVH * HD
    gain_one, gain_two = (
        lax.all_gather(attn_gain, "fs", axis=0, tiled=True),
        lax.all_gather(mlp_gain, "fs", axis=0, tiled=True),
    )
    query_full, pair_full, output_full, gate_full, upward_full, down_full = (
        spread_weight(w_query),
        spread_weight(w_kv),
        spread_weight(w_out),
        spread_weight(w_gate),
        spread_weight(w_up),
        spread_weight(w_down),
    )
    gain_one = gain_one.astype(jnp.float32)
    gain_two = gain_two.astype(jnp.float32)
    cosine, sine_table = rope_tables(positions)
    scale_one = rms_scale(tokens)
    normed_one = tokens * scale_one
    inputs_one = (normed_one * gain_one).astype(jnp.bfloat16)
    query_linear = jnp.dot(inputs_one, query_full, preferred_element_type=jnp.float32).reshape(
        row_count, HQ, HD
    )
    queries = (
        rotate(query_linear, cosine, sine_table)
        .astype(jnp.bfloat16)
        .reshape(row_count, query_width)
    )
    pair_linear = jnp.dot(inputs_one, pair_full, preferred_element_type=jnp.float32)
    keys_rotated = rotate(
        pair_linear[:, :key_width].reshape(row_count, KVH, HD), cosine, sine_table
    ).reshape(row_count, key_width)
    key_values = jnp.concatenate([keys_rotated, pair_linear[:, key_width:]], axis=1).astype(
        jnp.bfloat16
    )
    all_pairs = lax.all_gather(key_values, AXES, axis=0, tiled=True)
    starts = lax.all_gather(positions[:1] // TILE, AXES, axis=0, tiled=True)
    slots = jnp.zeros_like(starts).at[starts].set(jnp.arange(starts.shape[0], dtype=jnp.int32))
    own = positions[:1] // TILE
    query_pad = pad_heads(queries, 0)
    out_pad, logs = attend(query_pad, all_pairs, slots, own)
    attn_rows = unpad_heads(out_pad, KVH)
    attn_low = attn_rows.astype(jnp.bfloat16)
    middle = tokens + jnp.dot(attn_low, output_full, preferred_element_type=jnp.float32)
    scale_two = rms_scale(middle)
    normed_two = middle * scale_two
    inputs_two = (normed_two * gain_two).astype(jnp.bfloat16)
    gate_linear = jnp.dot(inputs_two, gate_full, preferred_element_type=jnp.float32)
    up_linear = jnp.dot(inputs_two, upward_full, preferred_element_type=jnp.float32)
    sigmoid_gate = jax.nn.sigmoid(gate_linear)
    activated = gate_linear * sigmoid_gate
    hidden = (activated * up_linear).astype(jnp.bfloat16)
    result = middle + jnp.dot(hidden, down_full, preferred_element_type=jnp.float32)
    grad_low = cotangent.astype(jnp.bfloat16)
    hidden_both, low_both = swap_tokens(hidden, 1), swap_whole(grad_low)
    down_sum = ctx_scatter(hidden_both, low_both)
    grad_hidden = jnp.dot(grad_low, down_full.T, preferred_element_type=jnp.float32)
    grad_gate_in = (
        grad_hidden * up_linear * sigmoid_gate * (1.0 + gate_linear * (1.0 - sigmoid_gate))
    ).astype(jnp.bfloat16)
    grad_up_in = (grad_hidden * activated).astype(jnp.bfloat16)
    inputs_two_both = swap_tokens(inputs_two, 8)
    gate_up_both = swap_whole(jnp.concatenate([grad_gate_in, grad_up_in], axis=1))
    gate_up_sum = ctx_scatter(inputs_two_both, gate_up_both)
    grad_inputs_two = jnp.dot(
        grad_gate_in, gate_full.T, preferred_element_type=jnp.float32
    ) + jnp.dot(grad_up_in, upward_full.T, preferred_element_type=jnp.float32)
    grad_norm_two, grad_mlp_gain = norm_back(grad_inputs_two, normed_two, scale_two, gain_two)
    grad_middle = cotangent + grad_norm_two
    grad_middle_low = grad_middle.astype(jnp.bfloat16)
    output_sum = ctx_scatter(swap_tokens(attn_low, 8), swap_whole(grad_middle_low))
    grad_attn = jnp.dot(grad_middle_low, output_full.T, preferred_element_type=jnp.float32).astype(
        jnp.bfloat16
    )
    delta_rows = jnp.sum(
        grad_attn.astype(jnp.float32).reshape(row_count, HQ, HD)
        * attn_rows.reshape(row_count, HQ, HD),
        axis=-1,
    )
    deltas = jnp.transpose(delta_rows.reshape(row_count, KVH, groups), (1, 2, 0)).reshape(
        KVH, 1, groups * row_count
    )
    dout_pad = pad_heads(grad_attn, KVH)
    grad_query_pad, term_rows = attend_back(
        query_pad, dout_pad, logs, deltas, all_pairs, slots, own
    )
    summed = lax.psum_scatter(term_rows, AXES, scatter_dimension=0, tiled=True).astype(jnp.float32)
    grad_keys = summed[:, :key_width].reshape(row_count, KVH, HD)
    grad_values = summed[:, key_width:].reshape(row_count, KVH, HD)
    grad_query_rows = unpad_heads(grad_query_pad, 0).reshape(row_count, HQ, HD)
    query_back = (
        rotate(grad_query_rows, cosine, -sine_table)
        .astype(jnp.bfloat16)
        .reshape(row_count, query_width)
    )
    key_back = rotate(grad_keys, cosine, -sine_table).reshape(row_count, key_width)
    pair_back = jnp.concatenate(
        [key_back, grad_values.reshape(row_count, key_width)], axis=1
    ).astype(jnp.bfloat16)
    back_sum = ctx_scatter(
        swap_tokens(inputs_one, 8),
        swap_whole(jnp.concatenate([query_back, pair_back], axis=1)),
    )
    grad_inputs_one = jnp.dot(
        query_back, query_full.T, preferred_element_type=jnp.float32
    ) + jnp.dot(pair_back, pair_full.T, preferred_element_type=jnp.float32)
    grad_norm_one, grad_attn_gain = norm_back(grad_inputs_one, normed_one, scale_one, gain_one)
    grad_tokens = grad_middle + grad_norm_one
    gains = lax.psum(jnp.stack([grad_attn_gain, grad_mlp_gain]), AXES)
    half_width = attn_gain.shape[0]
    gain_grads = lax.dynamic_slice(
        gains, (0, lax.axis_index("fs") * half_width), (2, half_width)
    )
    gate_up = ctx_gather(gate_up_sum, half_width)
    hidden_width = w_gate.shape[1]
    back = ctx_gather(back_sum, half_width)
    return (
        result,
        grad_tokens,
        gain_grads[0],
        back[:, :query_width],
        back[:, query_width:],
        ctx_gather(output_sum, w_out.shape[0]),
        gain_grads[1],
        gate_up[:, :hidden_width],
        gate_up[:, hidden_width:],
        ctx_gather(down_sum, w_down.shape[0]),
    )


def solution(mesh):
    parts, halves = mesh.shape["ctx"], mesh.shape["fs"]
    cores = 2 if parts % 2 == 0 else 1
    fine = jax.sharding.Mesh(mesh.devices.reshape(parts // cores, cores, halves), AXES)
    in_specs = (
        P(AXES, None),
        P(AXES),
        P("fs"),
        P("fs", None),
        P("fs", None),
        P("fs", None),
        P("fs"),
        P("fs", None),
        P("fs", None),
        P("fs", None),
        P(AXES, None),
    )
    out_specs = (
        P(AXES, None),
        P(AXES, None),
        P("fs"),
        P("fs", None),
        P("fs", None),
        P("fs", None),
        P("fs"),
        P("fs", None),
        P("fs", None),
        P("fs", None),
    )
    return jax.shard_map(shards, mesh=fine, in_specs=in_specs, out_specs=out_specs, check_vma=False)
```

time: 1530 us -> 901 us (0.59)
  waiting for transfers between devices: 888 us -> 605 us
  blocking collectives: 267 us -> 108 us
  loops' own time: 86.4 us -> 0 us
  other arithmetic: 104 us -> 21.1 us
  local copies, waits for them, and re-layouts: 91.7 us -> 35.3 us
  Pallas kernels: 0 us -> 53.2 us
    unnamed x26 -> x15, waiting for transfers between devices: 241 us -> 0.24 us
    reduce_scatter x7 -> x5, waiting for transfers between devices: 458 us -> 327 us  [the longest x4 201 us: ctx_scatter(): return lax.psum_scatter(partial, CTX, scatter_dimension=0, tiled=True)]
    all_gather x4 -> x1, blocking collectives: 143 us -> 22.9 us  [ctx_gather(): lax.all_gather(piece, CTX, axis=0, tiled=True)[:rows].astype(jnp.float32)]
    another operation x66 -> x0, loops' own time: 86.4 us -> none  [the longest x1 42.5 us: forward_piece(): lax.scan(forward_visit, carried, (pair_blocks, position_blocks))]
    reduce_min x64 -> x0, other arithmetic: 84.4 us -> none  [the longest x32 42.3 us: forward_visit(): active = jnp.min(block_positions) <= jnp.max(query_positions)]
    ppermute x0 -> x8, waiting for transfers between devices: none -> 60 us  [the longest x4 42.3 us: swap_tokens(): return jnp.concatenate([mine, lax.ppermute(theirs, 'fs', SWAP)], axis=0)]
    pallas_call x0 -> x2, Pallas kernels: none -> 53.2 us  [the longest x1 28.1 us: attend_back(): pl.pallas_call(functools.partial(backward_kernel, chunk_of(length // TILE...]
    unnamed x3 -> x2, blocking collectives: 92.2 us -> 46.1 us
  transfers between devices with their start and end apart: 22 -> 23, of which waited for: 15 -> 16; matrix products, arithmetic and copies ran while one was open for 21% -> 8% of each run, Pallas kernels for 0% -> 3%
where the time goes in v1:
time: 901 us; the launch traced here: 895 us
  waiting for transfers between devices  605 us (67%)
  blocking collectives  108 us (12%)
  Pallas kernels  53.2 us (6%)
  matrix products  47.8 us (5%)
  local copies, waits for them, and re-layouts  35.3 us (4%)
  other arithmetic  21.1 us (2%)
  between operations  15.8 us (2%)
  starting transfers between devices  9.14 us (1%)
    reduce_scatter x4, waiting for transfers between devices, ctx_scatter(): return lax.psum_scatter(partial, CTX, scatter_dimension=0, tiled=True)  201 us
    reduce_scatter x1, waiting for transfers between devices, shards(): lax.psum_scatter(term_rows, AXES, scatter_dimension=0, tiled=True)  126 us
    all_gather x6, waiting for transfers between devices, spread_weight(): return lax.all_gather(own, ('fs', 'core'), axis=0, tiled=True)  116 us
    all_gather x3, waiting for transfers between devices, ctx_gather(): lax.all_gather(piece, CTX, axis=0, tiled=True)[:rows].astype(jnp.float32)  67.2 us
    unnamed x2, blocking collectives  46.1 us
    ppermute x4, waiting for transfers between devices, swap_tokens(): return jnp.concatenate([mine, lax.ppermute(theirs, 'fs', SWAP)], axis=0)  42.3 us
    psum x1, blocking collectives, shards(): gains = lax.psum(jnp.stack([grad_attn_gain, grad_mlp_gain]), AXES)  39.4 us
    all_gather x1, waiting for transfers between devices, shards(): all_pairs = lax.all_gather(key_values, AXES, axis=0, tiled=True)  34.3 us
  transfers between devices with their start and end apart: 23, of which 16 were waited for; matrix products, arithmetic and copies ran while one was open for 8% of the time, Pallas kernels for 3%

profile of v1, /device:TPU:0, one launch (start us, length us, event | category | flops | bytes accessed | tf_op | source)
XLA Modules:
  0.0 895.4 jit_solution(13319839232697554770)
XLA Ops:
  12.9 6.4 all-reduce.6
  20.5 10.2 %all-gather.13.cloned.1.call-done = bf16[960,640]{1,0:T(8,128)(2,1)} async-done(((bf16[240,640]{1,0:T(8,128)(2,1)}), bf16[960,640]{1,0:T(8,128)(2,1)}) %all-gather.13.cloned.1.call-update) | async-done | bytes 1228816 | tf_op jit(solution)/shard_map/all_gather | solution.py:268
  43.6 39.7 %all-reduce.3 = s32[32]{0:T(128)S(1)} all-reduce(s32[32]{0:T(128)S(1)} %fusion.78), channel_id=1, replica_groups=mesh['chip'=8,'core'=2,'fs'=2] {'chip','core','fs'}, use_global_device_ids=true, to_apply=%add.3 | all-reduce | flops 32 | bytes 256
  89.7 34.3 %all-gather.15.cloned.1.call-done.pairs_ref = bf16[4096,640]{1,0:T(8,128)(2,1)} async-done(((bf16[128,640]{1,0:T(8,128)(2,1)}), bf16[4096,640]{1,0:T(8,128)(2,1)}) %all-gather.15.cloned.1.call-update) | async-done | bytes 5242896 | tf_op jit(solution)/shard_map/all_gather | solution.py:336
  124.0 25.1 %attend.1 = (f32[5,128,384]{2,1,0:T(8,128)}, f32[5,1,384]{2,1,0:T(1,128)}) custom-call(s32[32]{0:T(128)} %scatter_custom_fusion.slots_ref, s32[1]{0:T(128)} %and_select_fusion.1.own_ref, bf16[5,384,128]{2,1,0:T(8,128)(2,1)} %pad_maximum_fusion.2.query_ref, bf16[4096,640]{1,0:T(8,128)(2,1)} %all-gather.15.cloned.1.call-done.pairs_ref), custom_call_target="tpu_custom_call" | custom-call | flops 6039797760 | bytes 5242880 | tf_op jit(solution)/shard_map/attend/pallas_call | solution.py:198
  154.1 32.9 %all-gather.21.cloned.1.call-done = bf16[960,2560]{1,0:T(8,128)(2,1)} async-done(((bf16[240,2560]{1,0:T(8,128)(2,1)}), bf16[960,2560]{1,0:T(8,128)(2,1)}) %all-gather.21.cloned.1.call-update) | async-done | bytes 4915216 | tf_op jit(solution)/shard_map/all_gather | solution.py:268
  191.3 36.2 %all-gather.19.cloned.1.call-done = bf16[960,2560]{1,0:T(8,128)(2,1)} async-done(((bf16[240,2560]{1,0:T(8,128)(2,1)}), bf16[960,2560]{1,0:T(8,128)(2,1)}) %all-gather.19.cloned.1.call-update) | async-done | bytes 4915216 | tf_op jit(solution)/shard_map/all_gather | solution.py:268
  231.8 36.4 %all-gather.23.cloned.1.call-done = bf16[2560,960]{0,1:T(8,128)(2,1)} async-done(((bf16[640,960]{0,1:T(8,128)(2,1)}), bf16[2560,960]{0,1:T(8,128)(2,1)}) %all-gather.23.cloned.1.call-update) | async-done | bytes 4915216 | tf_op jit(solution)/shard_map/all_gather | solution.py:268
  268.2 5.5 multiply_convert_fusion
  285.9 28.1 %attend_back.1 = (f32[5,128,384]{2,1,0:T(8,128)}, bf16[4096,640]{1,0:T(8,128)(2,1)}) custom-call(s32[32]{0:T(128)} %scatter_custom_fusion.slots_ref, s32[1]{0:T(128)} %and_select_fusion.1.own_ref, bf16[5,384,128]{2,1,0:T(8,128)(2,1)} %pad_maximum_fusion.2.query_ref, bf16[5,384,128]{2,1,0:T(8,128)(2,1)} %pad_maximum_fusion.3.dout_ref, ...), custom_call_target="tpu_custom_call" | custom-call | flops 10066329600 | bytes 10485760 | tf_op jit(solution)/shard_map/attend_back/pallas_call | solution.py:225
  317.3 17.7 %collective-permute-done.7 = bf16[128,960]{0,1:T(8,128)(2,1)S(1)} collective-permute-done((bf16[128,960]{0,1:T(8,128)(2,1)S(1)}, bf16[128,960]{0,1:T(8,128)(2,1)S(1)}, u32[]{:S(2)}, u32[]{:S(2)}) %collective-permute-start.7) | collective-permute-done | bytes 245792 | tf_op jit(solution)/shard_map/ppermute | solution.py:272
  339.2 126.4 %reduce-scatter.6.cloned.1.call-done = bf16[128,640]{1,0:T(8,128)(2,1)} async-done(((bf16[4096,640]{1,0:T(8,128)(2,1)}), bf16[128,640]{1,0:T(8,128)(2,1)}) %reduce-scatter.6.cloned.1.call-update) | async-done | bytes 163856 | tf_op jit(solution)/shard_map/reduce_scatter | solution.py:387
  470.1 8.6 collective-permute-done
  484.2 28.1 %collective-permute-done.4 = bf16[128,512]{0,1:T(8,128)(2,1)S(1)} collective-permute-done((bf16[128,512]{0,1:T(8,128)(2,1)S(1)}, bf16[128,512]{0,1:T(8,128)(2,1)S(1)}, u32[]{:S(2)}, u32[]{:S(2)}) %collective-permute-start.4) | collective-permute-done | bytes 131104 | tf_op jit(solution)/shard_map/ppermute | solution.py:284
  512.3 7.0 convolution_convert_fusion
  522.2 5.6 collective-permute-done.2
  531.9 63.3 %reduce-scatter.8.cloned.1.call-done = bf16[32,1600]{1,0:T(8,128)(2,1)} async-done(((bf16[512,1600]{1,0:T(8,128)(2,1)}), bf16[32,1600]{1,0:T(8,128)(2,1)}) %reduce-scatter.8.cloned.1.call-update) | async-done | bytes 102416 | tf_op jit(solution)/shard_map/reduce_scatter | solution.py:289
  595.2 81.1 %reduce-scatter.12.cloned.1.call-done = bf16[32,5120]{1,0:T(8,128)(2,1)} async-done(((bf16[512,5120]{1,0:T(8,128)(2,1)}), bf16[32,5120]{1,0:T(8,128)(2,1)}) %reduce-scatter.12.cloned.1.call-update) | async-done | bytes 327696 | tf_op jit(solution)/shard_map/reduce_scatter | solution.py:289
  682.5 54.8 %reduce-scatter.10.cloned.1.call-done = bf16[32,960]{1,0:T(8,128)(2,1)} async-done(((bf16[512,960]{1,0:T(8,128)(2,1)}), bf16[32,960]{1,0:T(8,128)(2,1)}) %reduce-scatter.10.cloned.1.call-update) | async-done | bytes 61456 | tf_op jit(solution)/shard_map/reduce_scatter | solution.py:289
  737.3 22.9 %all_gather.53 = bf16[512,960]{1,0:T(8,128)(2,1)S(1)} all-gather(bf16[32,960]{1,0:T(8,128)(2,1)} %reduce-scatter.10.cloned.1.call-done), channel_id=1, replica_groups=mesh['chip'=8,'core'=2,'fs'=2] {'chip','core'}, dimensions={0}, use_global_device_ids=true | all-gather | bytes 1044480 | tf_op jit(solution)/shard_map/all_gather | solution.py:293
  761.8 20.7 %all-gather.29.cloned.1.call-done = bf16[1280,960]{1,0:T(8,128)(2,1)} async-done(((bf16[80,960]{1,0:T(8,128)(2,1)}), bf16[1280,960]{1,0:T(8,128)(2,1)}) %all-gather.29.cloned.1.call-update) | async-done | bytes 2457616 | tf_op jit(solution)/shard_map/all_gather | solution.py:293
  782.4 4.8 copy.56
  788.0 39.4 %psum.7 = f32[2,960]{1,0:T(2,128)S(1)} all-reduce(f32[2,960]{1,0:T(2,128)S(1)} %pad_maximum_fusion.9), channel_id=1, replica_groups=mesh['chip'=8,'core'=2,'fs'=2] {'chip','core','fs'}, use_global_device_ids=true, to_apply=%region_9.10 | all-reduce | flops 1920 | bytes 15360 | tf_op jit(solution)/shard_map/psum | solution.py:409
  833.7 46.5 %all-gather.27.cloned.1.call-done = bf16[512,5120]{1,0:T(8,128)(2,1)} async-done(((bf16[32,5120]{1,0:T(8,128)(2,1)}), bf16[512,5120]{1,0:T(8,128)(2,1)}) %all-gather.27.cloned.1.call-update) | async-done | bytes 5242896 | tf_op jit(solution)/shard_map/all_gather | solution.py:293
  (230 shorter events, 98.0 us)
Async XLA Ops:
  7.2 23.4 %all-gather.13.cloned.1.call-start = ((), (), s32[]{:S(2)}) async-start(), calls=%async_computation.6 | async-start | bytes 1536000 | tf_op jit(solution)/shard_map/all_gather | solution.py:268
  9.2 75.9 %all-gather.11.cloned.1.call-start = ((), (), s32[]{:S(2)}) async-start(), calls=%async_computation.5 | async-start | bytes 2457600 | tf_op jit(solution)/shard_map/all_gather | solution.py:268
  11.1 112.9 %all-gather.15.cloned.1.call-start = ((), (), s32[]{:S(2)}) async-start(), calls=%async_computation.7 | async-start | bytes 5406720 | tf_op jit(solution)/shard_map/all_gather | solution.py:336
  35.2 115.2 %all-gather.17.cloned.1.call-start = ((), (), s32[]{:S(2)}) async-start(), calls=%async_computation.8 | async-start | bytes 2457600 | tf_op jit(solution)/shard_map/all_gather | solution.py:268
  37.1 149.9 %all-gather.21.cloned.1.call-start = ((), (), s32[]{:S(2)}) async-start(), calls=%async_computation.10 | async-start | bytes 6144000 | tf_op jit(solution)/shard_map/all_gather | solution.py:268
  38.3 189.2 %all-gather.19.cloned.1.call-start = ((), (), s32[]{:S(2)}) async-start(), calls=%async_computation.9 | async-start | bytes 6144000 | tf_op jit(solution)/shard_map/all_gather | solution.py:268
  40.9 227.3 %all-gather.23.cloned.1.call-start = ((), (), s32[]{:S(2)}) async-start(), calls=%async_computation.11 | async-start | bytes 6144000 | tf_op jit(solution)/shard_map/all_gather | solution.py:268
  43.4 422.1 %reduce-scatter.6.cloned.1.call-start = ((), (), s32[]{:S(2)}) async-start(), calls=%async_computation.12 | async-start | bytes 5406720 | tf_op jit(solution)/shard_map/reduce_scatter | solution.py:387
  83.8 184.3 %copy-start.28 = (bf16[128,960]{0,1:T(8,128)(2,1)}, bf16[128,960]{0,1:T(8,128)(2,1)S(1)}, u32[]{:S(2)}) copy-start(bf16[128,960]{0,1:T(8,128)(2,1)S(1)} %convert_element_type.89) | copy-start | bytes 737284
  314.0 217.8 %reduce-scatter.14.cloned.1.call-start = ((), (), s32[]{:S(2)}) async-start(), calls=%async_computation.18 | async-start | bytes 2785280 | tf_op jit(solution)/shard_map/reduce_scatter | solution.py:289
  315.2 19.8 %collective-permute-start.6 = (bf16[128,1280]{1,0:T(8,128)(2,1)S(1)}, bf16[128,1280]{1,0:T(8,128)(2,1)S(1)}, u32[]{:S(2)}, u32[]{:S(2)}) collective-permute-start(bf16[128,1280]{1,0:T(8,128)(2,1)S(1)} %get-tuple-element.62), channel_id=1, source_target_pairs={{0,1},{1,0},{2,3},{3,2},{4,5},{5,4},{6,7},{7,6},{8,9},{9,8},{10,11... | collective-permute-start | bytes 983048 | tf_op jit(solution)/shard_map/ppermute | solution.py:284
  315.2 19.8 %collective-permute-start.7 = (bf16[128,960]{0,1:T(8,128)(2,1)S(1)}, bf16[128,960]{0,1:T(8,128)(2,1)S(1)}, u32[]{:S(2)}, u32[]{:S(2)}) collective-permute-start(bf16[128,960]{0,1:T(8,128)(2,1)S(1)} %copy-done.29), channel_id=1, source_target_pairs={{0,1},{1,0},{2,3},{3,2},{4,5},{5,4},{6,7},{7,6},{8,9},{9,8},{10,11... | collective-permute-start | bytes 737288 | tf_op jit(solution)/shard_map/ppermute | solution.py:272
  337.4 257.7 %reduce-scatter.8.cloned.1.call-start = ((), (), s32[]{:S(2)}) async-start(), calls=%async_computation.13 | async-start | bytes 1810432 | tf_op jit(solution)/shard_map/reduce_scatter | solution.py:289
  467.0 11.8 %collective-permute-start.1 = (bf16[128,1600]{0,1:T(8,128)(2,1)S(1)}, bf16[128,1600]{0,1:T(8,128)(2,1)S(1)}, u32[]{:S(2)}, u32[]{:S(2)}) collective-permute-start(bf16[128,1600]{0,1:T(8,128)(2,1)S(1)} %pad_maximum_fusion.4), channel_id=1, source_target_pairs={{0,1},{1,0},{2,3},{3,2},{4,5},{5,4},{6,7},{7,6},{8,9},{9,8},{10,11... | collective-permute-start | bytes 1228808 | tf_op jit(solution)/shard_map/ppermute | solution.py:272
  468.1 10.6 %collective-permute-start = (bf16[128,512]{0,1:T(8,128)(2,1)S(1)}, bf16[128,512]{0,1:T(8,128)(2,1)S(1)}, u32[]{:S(2)}, u32[]{:S(2)}) collective-permute-start(bf16[128,512]{0,1:T(8,128)(2,1)S(1)} %get-tuple-element.90), channel_id=1, source_target_pairs={{0,1},{1,0},{2,3},{3,2},{4,5},{5,4},{6,7},{7,6},{8,9},{9,8},{10,11... | collective-permute-start | bytes 393224 | tf_op jit(solution)/shard_map/ppermute | solution.py:284
  480.7 195.7 %reduce-scatter.12.cloned.1.call-start = ((), (), s32[]{:S(2)}) async-start(), calls=%async_computation.16 | async-start | bytes 5570560 | tf_op jit(solution)/shard_map/reduce_scatter | solution.py:289
  482.1 30.2 %collective-permute-start.5 = (bf16[128,5120]{1,0:T(8,128)(2,1)S(1)}, bf16[128,5120]{1,0:T(8,128)(2,1)S(1)}, u32[]{:S(2)}, u32[]{:S(2)}) collective-permute-start(bf16[128,5120]{1,0:T(8,128)(2,1)S(1)} %pad_maximum_fusion), channel_id=1, source_target_pairs={{0,1},{1,0},{2,3},{3,2},{4,5},{5,4},{6,7},{7,6},{8,9},{9,8},{10,11... | collective-permute-start | bytes 3932168 | tf_op jit(solution)/shard_map/ppermute | solution.py:272
  482.4 29.9 %collective-permute-start.4 = (bf16[128,512]{0,1:T(8,128)(2,1)S(1)}, bf16[128,512]{0,1:T(8,128)(2,1)S(1)}, u32[]{:S(2)}, u32[]{:S(2)}) collective-permute-start(bf16[128,512]{0,1:T(8,128)(2,1)S(1)} %get-tuple-element.72), channel_id=1, source_target_pairs={{0,1},{1,0},{2,3},{3,2},{4,5},{5,4},{6,7},{7,6},{8,9},{9,8},{10,11... | collective-permute-start | bytes 393224 | tf_op jit(solution)/shard_map/ppermute | solution.py:284
  519.3 218.0 %reduce-scatter.10.cloned.1.call-start = ((), (), s32[]{:S(2)}) async-start(), calls=%async_computation.15 | async-start | bytes 1114112 | tf_op jit(solution)/shard_map/reduce_scatter | solution.py:289
  520.2 7.6 collective-permute-start.3
  520.8 7.0 collective-permute-start.2
  530.2 252.3 %all-gather.29.cloned.1.call-start = ((), (), s32[]{:S(2)}) async-start(), calls=%async_computation.19 | async-start | bytes 2785280 | tf_op jit(solution)/shard_map/all_gather | solution.py:293
  531.8 297.3 %all-gather.25.cloned.1.call-start = ((), (), s32[]{:S(2)}) async-start(), calls=%async_computation.14 | async-start | bytes 1810432 | tf_op jit(solution)/shard_map/all_gather | solution.py:293
  595.2 285.0 %all-gather.27.cloned.1.call-start = ((), (), s32[]{:S(2)}) async-start(), calls=%async_computation.17 | async-start | bytes 5570560 | tf_op jit(solution)/shard_map/all_gather | solution.py:293
  (44 other events, 1165.9 us)
Sparse Core Ops, SparseCore 0:
  10.2 20.4 all-gather.12
  32.8 22.3 all-gather.10
  58.6 65.3 all-gather.14
  126.0 20.3 all-gather.16
  148.3 38.5 all-gather.20
  188.9 38.4 all-gather.18
  229.6 38.4 all-gather.22
  314.2 151.3 reduce-scatter.5
  469.9 61.8 reduce-scatter.13
  535.9 59.2 reduce-scatter.7
  599.0 77.3 reduce-scatter.11
  680.4 56.8 reduce-scatter.9
  739.6 42.7 all-gather.28
  784.6 38.7 all-gather.24
  825.6 54.5 all-gather.26
